TPU v7x, 512 devices: a whole 4x4x16 slice. The times are simulated.
512 devices in a mesh: axial: 64 (over z, x), azim: 8 (over y, core).
Axes of the slice: x: 4, y: 4, z: 16, core: 2. Of those that a mesh axis runs over, the one named last changes fastest.
Arguments:
- state: float32 [14, 512, 64, 128], P(None, 'axial', 'azim'), may hold values from -18 to 18, as said below
- diff_coef: float32 [10], replicated, may hold values from 0.1 to 1
- parcel_state: float32 [8, 1048576], P(None, ('axial', 'azim')), may hold values from -6 to 6, as said below
- parcel_cell: int32 [1048576], P(('axial', 'azim')), may hold values from 0 to 8191
- parcel_dest: int32 [1048576], P(('axial', 'azim')), may hold values from 0 to 4, as said below
- live_count: int32 [512], P(('axial', 'azim')), may hold values from 256 to 2048, as said below
Outputs:
- scalars_new: float32 [10, 512, 64, 128], P(None, 'axial', 'azim')
- velocity_new: float32 [3, 512, 64, 128], P(None, 'axial', 'azim')
- kept_parcels: float32 [8, 1048576], P(None, ('axial', 'azim'))
- arrived: float32 [4, 8, 32768], P(None, None, ('axial', 'azim'))
Inputs may be any that keep to these rules, and one draw needn't show every extreme that they name: `state`: component 0 (density) lies in [0.5, 2] and components 5 to 13 (species fractions) in [0, 1]. `parcel_state`: row 0 (mass) lies in [0.2, 2], rows 5 to 7 (offsets) in [0, 1]. Live parcels of a box fill its first live_count slots; boxes at axial index 0 are full. `parcel_dest`: among the live parcels of one box at most 64 have any one destination 1 to 4, and in every box one destination has exactly 64. Entries of slots that are not live are ignored. `parcel_cell`: x * 8 * 128 + y * 128 + z for box-local cell (x, y, z).
All inputs are finite; a program needn't handle non-finite values. Where the computation divides by a largest or mean magnitude, that divisor is 1e-20 or more.
Results may differ from a plain program's by a relative error of at most 0.0003.
Values sent between devices are 32-bit elements; how exact they have to be, the bound alone decides.
A program may use at most 64 MiB of HBM per device.

v0:
```python
import jax
import jax.numpy as jnp
from jax import lax
from jax.sharding import PartitionSpec as P

CAP = 64
ITERS = 4
CFL = 0.4
SHIFT_PRESSURE = 0.25
EVAP = 8.0
RELAX = 4.0
DRAG = 6.0
LATENT = 0.5
HEAT_CAP = 0.8
HIGHEST = lax.Precision.HIGHEST


def extended(block, sides, width):
    for axis, dim in sides:
        count = lax.axis_size(axis)
        forward = [(i, i + 1) for i in range(count - 1)]
        forward.append((count - 1, 0))
        backward = [(target, source) for source, target in forward]
        low = lax.ppermute(
            lax.slice_in_dim(block, block.shape[dim] - width, None, axis=dim), axis, forward
        )
        high = lax.ppermute(lax.slice_in_dim(block, 0, width, axis=dim), axis, backward)
        block = jnp.concatenate([low, block, high], axis=dim)
    return block


def shifted_2(shard, axis, by):
    length = lax.axis_size(axis)
    pairs = [(i, i + by) for i in range(length) if 0 <= i + by < length]
    return lax.ppermute(shard, axis, pairs)


def shifted_3(shard, axis, by):
    length = lax.axis_size(axis)
    return lax.ppermute(shard, axis, [(i, (i + by) % length) for i in range(length)])


def shifted(padded, rim_width, direction, step_by):
    selector = []
    total_dims = padded.ndim
    for dim_index in range(total_dims):
        extent = padded.shape[dim_index]
        if dim_index == total_dims - 3 + direction:
            selector.append(slice(rim_width + step_by, extent - rim_width + step_by))
        elif dim_index >= total_dims - 3:
            selector.append(slice(rim_width, extent - rim_width))
        else:
            selector.append(slice(None))
    return padded[tuple(selector)]


def clear_ends(padded, rim_width, axial_dim):
    extent = padded.shape[axial_dim]
    at_first = lax.axis_index("axial") == 0
    at_last = lax.axis_index("axial") == lax.axis_size("axial") - 1
    shape_list = [1] * padded.ndim
    shape_list[axial_dim] = extent
    position = lax.broadcasted_iota(jnp.int32, tuple(shape_list), axial_dim)
    dropped = at_first & (position < rim_width) | at_last & (position >= extent - rim_width)
    return jnp.where(dropped, jnp.float32(0.0), padded)


def radial_pad(values, rim_width, radial_mode):
    return jnp.pad(
        values, [(0, 0)] * (values.ndim - 1) + [(rim_width, rim_width)], mode=radial_mode
    )


def transport(scalar_pad, vel_pad, density_pad, density_rim, diffusion, step_size):
    center = shifted(scalar_pad, 2, 0, 0)
    density = shifted(density_pad, density_rim, 0, 0)
    change = jnp.zeros_like(center)
    for direction in range(3):
        carried = vel_pad[direction] * scalar_pad
        advect = (
            -shifted(carried, 2, direction, 2)
            + 8.0 * shifted(carried, 2, direction, 1)
            - 8.0 * shifted(carried, 2, direction, -1)
            + shifted(carried, 2, direction, -2)
        ) / 12.0
        upper_flux = (
            0.5
            * diffusion
            * (density + shifted(density_pad, density_rim, direction, 1))
            * (shifted(scalar_pad, 2, direction, 1) - center)
        )
        lower_flux = (
            0.5
            * diffusion
            * (density + shifted(density_pad, density_rim, direction, -1))
            * (center - shifted(scalar_pad, 2, direction, -1))
        )
        change = change - advect + upper_flux - lower_flux
    return center + step_size * change


def evaporate(attrs, gas_values, alive_mask, step_size):
    parcel_mass = attrs[0]
    parcel_temp = attrs[1]
    parcel_vel = attrs[2:5]
    offsets = attrs[5:8]
    gas_heat = gas_values[3]
    gas_fuel = gas_values[4]
    evap_rate = EVAP * jax.nn.softplus(gas_heat - parcel_temp) * (1.0 - gas_fuel)
    new_mass = parcel_mass * jnp.exp(-step_size * evap_rate)
    lost_mass = parcel_mass - new_mass
    new_temp = parcel_temp + step_size * RELAX * (gas_heat - parcel_temp)
    new_vel = parcel_vel + step_size * DRAG * (gas_values[0:3] - parcel_vel)
    new_offsets = offsets + step_size * new_vel
    heat_source = -LATENT * lost_mass - HEAT_CAP * new_mass * (new_temp - parcel_temp)
    new_attrs = (
        jnp.concatenate([new_mass[None], new_temp[None], new_vel, new_offsets], axis=0)
        * alive_mask[None]
    )
    sources = jnp.stack([heat_source * alive_mask, lost_mass * alive_mask])
    return (new_attrs, sources)


def pressure_pad(values):
    padded = extended(values, (("axial", 0), ("azim", 1)), 1)
    return radial_pad(clear_ends(padded, 1, 0), 1, "constant")


def operate(values):
    padded = pressure_pad(values)
    beside = shifted(padded, 1, 0, 1) + shifted(padded, 1, 0, -1)
    beside = beside + shifted(padded, 1, 1, 1) + shifted(padded, 1, 1, -1)
    beside = beside + shifted(padded, 1, 2, 1) + shifted(padded, 1, 2, -1)
    return (6.0 + SHIFT_PRESSURE) * values - beside


def neighbour_sum(padded):
    beside = shifted(padded, 1, 0, 1) + shifted(padded, 1, 0, -1)
    beside = beside + shifted(padded, 1, 1, 1) + shifted(padded, 1, 1, -1)
    return beside + shifted(padded, 1, 2, 1) + shifted(padded, 1, 2, -1)


def solve_pressure(divergence):
    half_width = 6.0
    basis = [divergence]
    padded_basis = []
    for j in range(ITERS):
        padded = pressure_pad(basis[j])
        padded_basis.append(padded)
        scaled = neighbour_sum(padded) * (-1.0 / half_width)
        if j == 0:
            basis.append(scaled)
        else:
            basis.append(2.0 * scaled - basis[j - 1])
    size = ITERS + 1
    pairs = [(i, j) for i in range(size) for j in range(i, size)]
    local = jnp.stack([jnp.sum(basis[i] * basis[j]) for i, j in pairs])
    total = lax.psum(local, ("axial", "azim"))
    gram = [[None] * size for _ in range(size)]
    for n, (i, j) in enumerate(pairs):
        gram[i][j] = total[n]
        gram[j][i] = total[n]
    shift = 6.0 + SHIFT_PRESSURE

    def apply_a(c):
        out = [shift * c[j] for j in range(size)]
        for j in range(size - 1):
            if j == 0:
                out[1] = out[1] + half_width * c[0]
            else:
                out[j + 1] = out[j + 1] + 0.5 * half_width * c[j]
                out[j - 1] = out[j - 1] + 0.5 * half_width * c[j]
        return out

    def inner(a, b):
        acc = None
        for i in range(size):
            for j in range(size):
                if isinstance(a[i], float) and a[i] == 0.0:
                    continue
                if isinstance(b[j], float) and b[j] == 0.0:
                    continue
                term = a[i] * gram[i][j] * b[j]
                acc = term if acc is None else acc + term
        return acc

    zero = 0.0
    solution_c = [zero] * size
    residual = [1.0] + [zero] * (size - 1)
    search = list(residual)
    norm_now = inner(residual, residual)
    for iteration in range(ITERS):
        image = apply_a(search)
        alpha = norm_now / inner(search, image)
        solution_c = [solution_c[j] + alpha * search[j] for j in range(size)]
        residual = [residual[j] - alpha * image[j] for j in range(size)]
        if iteration == ITERS - 1:
            break
        norm_next = inner(residual, residual)
        search = [residual[j] + norm_next / norm_now * search[j] for j in range(size)]
        norm_now = norm_next
    pressure = solution_c[0] * basis[0]
    padded_pressure = solution_c[0] * padded_basis[0]
    for j in range(1, ITERS):
        pressure = pressure + solution_c[j] * basis[j]
        padded_pressure = padded_pressure + solution_c[j] * padded_basis[j]
    return (pressure, padded_pressure)


def along_axial(buffer, step_by):
    return shifted_2(buffer, "axial", step_by)


def along_azim(buffer, step_by):
    return shifted_3(buffer, "azim", step_by)


def on_device(state, diff_coef, parcel_state, parcel_cell, parcel_dest, live_count):
    velocity = state[1:4]
    fastest = lax.pmax(jnp.max(jnp.abs(velocity)), ("axial", "azim"))
    step_size = CFL / (fastest + 1e-06)
    whole_pad = extended(state, (("axial", 1), ("azim", 2)), 2)
    whole_pad = radial_pad(clear_ends(whole_pad, 2, 1), 2, "edge")
    moving = whole_pad[1:]
    density_pad = whole_pad[0]
    density_rim = 2
    vel_pad = moving[0:3]
    transported = transport(
        moving[3:], vel_pad, density_pad, density_rim, diff_coef[:, None, None, None], step_size
    )
    npar_local = parcel_cell.shape[0]
    block_rows = 512
    cells_x, cells_y, cells_z = (state.shape[1], state.shape[2], state.shape[3])
    plane_count = cells_x * cells_y
    gas_table = jnp.transpose(state[1:6].reshape(5, plane_count, cells_z), (1, 0, 2)).reshape(
        plane_count, 5 * cells_z
    )
    live_now = live_count[0]

    def one_block(block_index, carried_pair):
        deposit, updated = carried_pair
        first_slot = block_index * block_rows
        cell_ids = lax.dynamic_slice_in_dim(parcel_cell, first_slot, block_rows)
        attrs = lax.dynamic_slice_in_dim(parcel_state, first_slot, block_rows, 1)
        alive_mask = (first_slot + jnp.arange(block_rows) < live_now).astype(jnp.float32)
        plane_ids = cell_ids // cells_z
        radial_ids = cell_ids % cells_z
        plane_hot = (plane_ids[:, None] == jnp.arange(plane_count)[None, :]).astype(jnp.float32)
        radial_hot = (radial_ids[:, None] == jnp.arange(cells_z)[None, :]).astype(jnp.float32)
        gas_rows = jnp.dot(plane_hot, gas_table, precision=HIGHEST).reshape(block_rows, 5, cells_z)
        gas_values = jnp.sum(gas_rows * radial_hot[:, None, :], axis=2).T
        new_attrs, sources = evaporate(attrs, gas_values, alive_mask, step_size)
        spread = (sources.T[:, :, None] * radial_hot[:, None, :]).reshape(block_rows, 2 * cells_z)
        deposit = deposit + lax.dot_general(
            plane_hot, spread, (((0,), (0,)), ((), ())), precision=HIGHEST
        )
        updated = lax.dynamic_update_slice_in_dim(updated, new_attrs, first_slot, 1)
        return (deposit, updated)

    initial = (jnp.zeros((plane_count, 2 * cells_z), jnp.float32), jnp.zeros_like(parcel_state))
    block_count = npar_local // block_rows
    deposit, updated = lax.fori_loop(0, block_count, one_block, initial)
    deposit = jnp.transpose(deposit.reshape(cells_x, cells_y, 2, cells_z), (2, 0, 1, 3))
    scalars_new = jnp.concatenate(
        [transported[:2] + deposit / state[0][None], transported[2:]], axis=0
    )
    slot_alive = jnp.arange(npar_local) < live_now
    stacked = jnp.stack([(parcel_dest == d + 1) & slot_alive for d in range(4)]).astype(jnp.int32)
    ranks = jnp.cumsum(stacked, axis=1) - 1
    mover = jnp.sum(stacked, axis=0) > 0
    target = jnp.where(mover, jnp.sum(stacked * (jnp.arange(4)[:, None] * CAP + ranks), axis=0), -1)
    select = (target[:, None] == jnp.arange(4 * CAP)[None, :]).astype(jnp.float32)
    buffers = jnp.transpose(
        jnp.dot(updated, select, precision=HIGHEST).reshape(updated.shape[0], 4, CAP), (1, 0, 2)
    )
    arrived = jnp.stack(
        [
            along_axial(buffers[0], -1),
            along_axial(buffers[1], 1),
            along_azim(buffers[2], -1),
            along_azim(buffers[3], 1),
        ]
    )
    kept_parcels = jnp.where((parcel_dest == 0)[None], updated, jnp.float32(0.0))
    divergence = jnp.zeros_like(state[0])
    for direction in range(3):
        divergence = divergence + 0.5 * (
            shifted(vel_pad[direction], 2, direction, 1)
            - shifted(vel_pad[direction], 2, direction, -1)
        )
    pressure, padded_pressure = solve_pressure(divergence)
    velocity_new = jnp.stack(
        [
            velocity[d]
            - 0.5 * (shifted(padded_pressure, 1, d, 1) - shifted(padded_pressure, 1, d, -1))
            for d in range(3)
        ]
    )
    return (scalars_new, velocity_new, kept_parcels, arrived)


def solution(mesh):
    in_specs = (
        P(None, "axial", "azim", None),
        P(),
        P(None, ("axial", "azim")),
        P(("axial", "azim")),
        P(("axial", "azim")),
        P(("axial", "azim")),
    )
    out_specs = (
        P(None, "axial", "azim", None),
        P(None, "axial", "azim", None),
        P(None, ("axial", "azim")),
        P(None, None, ("axial", "azim")),
    )
    return jax.shard_map(
        on_device, mesh=mesh, in_specs=in_specs, out_specs=out_specs, check_vma=False
    )
```

profile of v0, /device:TPU:1, one launch (start us, length us, event | category | flops | bytes accessed | tf_op | source)
XLA Modules:
  0.0 444.3 jit_solution(8661759650428608741)
XLA Ops:
  1.6 3.9 collective-permute-start
  5.6 12.1 %collective-permute-start.1 = (f32[14,2,8,128]{3,2,1,0:T(8,128)S(1)}, f32[14,2,8,128]{3,2,1,0:T(8,128)S(1)}, u32[]{:S(2)}, u32[]{:S(2)}) collective-permute-start(f32[14,2,8,128]{3,2,1,0:T(8,128)S(1)} %get-tuple-element.334), channel_id=1, source_target_pairs={{8,0},{16,8},{24,16},{32,24},{40,32},{48,40},{56,48},{64,56},{72,6... | collective-permute-start | bytes 344072 | tf_op jit(solution)/shard_map/ppermute | solution.py:27
  20.2 101.0 %pmax.7 = f32[]{:T(128)} all-reduce(f32[]{:T(128)} %abs_reduce_fusion), channel_id=1, replica_groups=mesh['axial'=64,'azim'=8] {'axial','azim'}, use_global_device_ids=true, to_apply=%region_1.0 | all-reduce | flops 1 | bytes 8 | tf_op jit(solution)/shard_map/pmax | solution.py:220
  122.6 31.6 %while.18 = (s32[]{:T(128)}, f32[64,256]{1,0:T(8,128)S(1)}, f32[8,2048]{1,0:T(8,128)S(1)}, s32[2048]{0:T(1024)}, s32[]{:T(128)}, /*index=5*/f32[8,2048]{1,0:T(8,...) while((s32[]{:T(128)}, f32[64,256]{1,0:T(8,128)S(1)}, ...), condition=%wide.region_4.5_spmd.clone, body=%wide.region_2.4_spmd.clone.sunk | while | flops 353384960 | bytes 5411153 | solution.py:262
  158.1 2.0 collective-permute-start.21
  161.0 3.2 collective-permute-start.3
  168.4 2.7 copy.247
  174.0 3.8 collective-permute-start.5
  177.8 1.9 collective-permute-start.4
  179.8 5.7 %collective-permute-done.4 = f32[1,8,128]{2,1,0:T(8,128)S(1)} collective-permute-done((f32[1,8,128]{2,1,0:T(8,128)S(1)}, f32[1,8,128]{2,1,0:T(8,128)S(1)}, u32[]{:S(2)}, u32[]{:S(2)}) %collective-permute-start.4) | collective-permute-done | bytes 4128 | tf_op jit(solution)/shard_map/ppermute | solution.py:24
  185.5 5.2 %collective-permute-start.7 = (f32[10,1,128]{2,1,0:T(1,128)S(1)}, f32[10,1,128]{2,1,0:T(1,128)S(1)}, u32[]{:S(2)}, u32[]{:S(2)}) collective-permute-start(f32[10,1,128]{2,1,0:T(1,128)S(1)} %get-tuple-element.349), channel_id=1, source_target_pairs={{1,0},{2,1},{3,2},{4,3},{5,4},{6,5},{7,6},{0,7},{9,8},{10,9},{11,1... | collective-permute-start | bytes 15368 | tf_op jit(solution)/shard_map/ppermute | solution.py:27
  192.9 1.9 collective-permute-start.9
  194.9 4.0 collective-permute-start.8
  199.5 3.0 collective-permute-done.8
  202.6 3.3 collective-permute-start.11
  207.2 2.6 collective-permute-start.13
  209.8 2.7 collective-permute-start.12
  213.5 4.0 collective-permute-done.12
  217.5 5.0 %collective-permute-start.15 = (f32[10,1,128]{2,1,0:T(1,128)S(1)}, f32[10,1,128]{2,1,0:T(1,128)S(1)}, u32[]{:S(2)}, u32[]{:S(2)}) collective-permute-start(f32[10,1,128]{2,1,0:T(1,128)S(1)} %get-tuple-element.345), channel_id=1, source_target_pairs={{1,0},{2,1},{3,2},{4,3},{5,4},{6,5},{7,6},{0,7},{9,8},{10,9},{11,1... | collective-permute-start | bytes 15368 | tf_op jit(solution)/shard_map/ppermute | solution.py:27
  225.9 3.5 collective-permute-start.16
  230.8 2.7 collective-permute-done.16
  233.5 4.3 collective-permute-start.19
  239.9 9.3 %stack.131 = f32[15]{0:T(128)S(1)} concatenate(f32[1]{0:T(128)} %bitcast.15, f32[1]{0:T(128)} %bitcast.16, f32[1]{0:T(128)} %bitcast.17, f32[1]{0:T(128)} %bitcast.18, f32[1]{0:T(128)} %bitcast.19, f32[1]{0:T(128)} %bitcast.20, f32[1]{0:T(128)} %bitcast.21, f32[1]{0:T(128)} %bitcast.22, f32[1]{0:T(128)} %bitcast.23, f32[1]{0:T(128)} %bitcast.24, f32[1]{0:T(128)} %bitcast.25, ...), dimensions={0} | concatenate | bytes 120 | tf_op jit(solution)/shard_map/stack | solution.py:157
  250.0 100.6 %psum.7 = f32[15]{0:T(128)S(1)} all-reduce(f32[15]{0:T(128)S(1)} %stack.131), channel_id=1, replica_groups=mesh['axial'=64,'azim'=8] {'axial','azim'}, use_global_device_ids=true, to_apply=%region_20.21 | all-reduce | flops 15 | bytes 120 | tf_op jit(solution)/shard_map/psum | solution.py:158
  (167 shorter events, 61.4 us)
Async XLA Ops:
  1.6 159.1 %collective-permute-start = (f32[14,2,8,128]{3,2,1,0:T(8,128)S(1)}, f32[14,2,8,128]{3,2,1,0:T(8,128)S(1)}, u32[]{:S(2)}, u32[]{:S(2)}) collective-permute-start(f32[14,2,8,128]{3,2,1,0:T(8,128)S(1)} %get-tuple-element.335), channel_id=1, source_target_pairs={{0,8},{8,16},{16,24},{24,32},{32,40},{40,48},{48,56},{56,64},{64,7... | collective-permute-start | bytes 344072 | tf_op jit(solution)/shard_map/ppermute | solution.py:24
  5.6 155.3 %collective-permute-start.1 = (f32[14,2,8,128]{3,2,1,0:T(8,128)S(1)}, f32[14,2,8,128]{3,2,1,0:T(8,128)S(1)}, u32[]{:S(2)}, u32[]{:S(2)}) collective-permute-start(f32[14,2,8,128]{3,2,1,0:T(8,128)S(1)} %get-tuple-element.334), channel_id=1, source_target_pairs={{8,0},{16,8},{24,16},{32,24},{40,32},{48,40},{56,48},{64,56},{72,6... | collective-permute-start | bytes 344072 | tf_op jit(solution)/shard_map/ppermute | solution.py:27
  157.1 37.8 %collective-permute-start.23 = (f32[8,64]{1,0:T(8,128)S(1)}, f32[8,64]{1,0:T(8,128)S(1)}, u32[]{:S(2)}, u32[]{:S(2)}) collective-permute-start(f32[8,64]{1,0:T(8,128)S(1)} %get-tuple-element.359), channel_id=1, source_target_pairs={{0,1},{1,2},{2,3},{3,4},{4,5},{5,6},{6,7},{7,0},{8,9},{9,10},{10,1... | collective-permute-start | bytes 6152 | tf_op jit(solution)/shard_map/ppermute | solution.py:40
  158.1 40.8 %collective-permute-start.22 = (f32[8,64]{1,0:T(8,128)S(1)}, f32[8,64]{1,0:T(8,128)S(1)}, u32[]{:S(2)}, u32[]{:S(2)}) collective-permute-start(f32[8,64]{1,0:T(8,128)S(1)} %get-tuple-element.360), channel_id=1, source_target_pairs={{0,7},{1,0},{2,1},{3,2},{4,3},{5,4},{6,5},{7,6},{8,15},{9,8},{10,9... | collective-permute-start | bytes 6152 | tf_op jit(solution)/shard_map/ppermute | solution.py:40
  158.1 40.8 %collective-permute-start.21 = (f32[8,64]{1,0:T(8,128)S(1)}, f32[8,64]{1,0:T(8,128)S(1)}, u32[]{:S(2)}, u32[]{:S(2)}) collective-permute-start(f32[8,64]{1,0:T(8,128)S(1)} %get-tuple-element.361), channel_id=1, source_target_pairs={{0,8},{8,16},{16,24},{24,32},{32,40},{40,48},{48,56},{56,64},{64,7... | collective-permute-start | bytes 6152 | tf_op jit(solution)/shard_map/ppermute | solution.py:35
  161.0 4.8 %collective-permute-start.3 = (f32[14,12,2,128]{3,2,1,0:T(2,128)S(1)}, f32[14,12,2,128]{3,2,1,0:T(2,128)S(1)}, u32[]{:S(2)}, u32[]{:S(2)}) collective-permute-start(f32[14,12,2,128]{3,2,1,0:T(2,128)S(1)} %get-tuple-element.330), channel_id=1, source_target_pairs={{1,0},{2,1},{3,2},{4,3},{5,4},{6,5},{7,6},{0,7},{9,8},{10,9},{11,1... | collective-permute-start | bytes 516104 | tf_op jit(solution)/shard_map/ppermute | solution.py:27
  164.2 2.4 collective-permute-start.2
  174.0 5.8 %collective-permute-start.5 = (f32[1,8,128]{2,1,0:T(8,128)S(1)}, f32[1,8,128]{2,1,0:T(8,128)S(1)}, u32[]{:S(2)}, u32[]{:S(2)}) collective-permute-start(f32[1,8,128]{2,1,0:T(8,128)S(1)} %get-tuple-element.357), channel_id=1, source_target_pairs={{8,0},{16,8},{24,16},{32,24},{40,32},{48,40},{56,48},{64,56},{72,6... | collective-permute-start | bytes 12296 | tf_op jit(solution)/shard_map/ppermute | solution.py:27
  177.8 7.7 %collective-permute-start.4 = (f32[1,8,128]{2,1,0:T(8,128)S(1)}, f32[1,8,128]{2,1,0:T(8,128)S(1)}, u32[]{:S(2)}, u32[]{:S(2)}) collective-permute-start(f32[1,8,128]{2,1,0:T(8,128)S(1)} %get-tuple-element.356), channel_id=1, source_target_pairs={{0,8},{8,16},{16,24},{24,32},{32,40},{40,48},{48,56},{56,64},{64,7... | collective-permute-start | bytes 12296 | tf_op jit(solution)/shard_map/ppermute | solution.py:24
  185.5 6.0 %collective-permute-start.7 = (f32[10,1,128]{2,1,0:T(1,128)S(1)}, f32[10,1,128]{2,1,0:T(1,128)S(1)}, u32[]{:S(2)}, u32[]{:S(2)}) collective-permute-start(f32[10,1,128]{2,1,0:T(1,128)S(1)} %get-tuple-element.349), channel_id=1, source_target_pairs={{1,0},{2,1},{3,2},{4,3},{5,4},{6,5},{7,6},{0,7},{9,8},{10,9},{11,1... | collective-permute-start | bytes 15368 | tf_op jit(solution)/shard_map/ppermute | solution.py:27
  190.6 2.1 collective-permute-start.6
  191.5 7.4 %collective-permute-start.20 = (f32[8,64]{1,0:T(8,128)S(1)}, f32[8,64]{1,0:T(8,128)S(1)}, u32[]{:S(2)}, u32[]{:S(2)}) collective-permute-start(f32[8,64]{1,0:T(8,128)S(1)} %get-tuple-element.358), channel_id=1, source_target_pairs={{8,0},{16,8},{24,16},{32,24},{40,32},{48,40},{56,48},{64,56},{72,6... | collective-permute-start | bytes 6152 | tf_op jit(solution)/shard_map/ppermute | solution.py:35
  192.9 6.6 %collective-permute-start.9 = (f32[1,8,128]{2,1,0:T(8,128)S(1)}, f32[1,8,128]{2,1,0:T(8,128)S(1)}, u32[]{:S(2)}, u32[]{:S(2)}) collective-permute-start(f32[1,8,128]{2,1,0:T(8,128)S(1)} %get-tuple-element.355), channel_id=1, source_target_pairs={{8,0},{16,8},{24,16},{32,24},{40,32},{48,40},{56,48},{64,56},{72,6... | collective-permute-start | bytes 12296 | tf_op jit(solution)/shard_map/ppermute | solution.py:27
  194.9 7.7 %collective-permute-start.8 = (f32[1,8,128]{2,1,0:T(8,128)S(1)}, f32[1,8,128]{2,1,0:T(8,128)S(1)}, u32[]{:S(2)}, u32[]{:S(2)}) collective-permute-start(f32[1,8,128]{2,1,0:T(8,128)S(1)} %get-tuple-element.354), channel_id=1, source_target_pairs={{0,8},{8,16},{16,24},{24,32},{32,40},{40,48},{48,56},{56,64},{64,7... | collective-permute-start | bytes 12296 | tf_op jit(solution)/shard_map/ppermute | solution.py:24
  202.6 4.5 %collective-permute-start.11 = (f32[10,1,128]{2,1,0:T(1,128)S(1)}, f32[10,1,128]{2,1,0:T(1,128)S(1)}, u32[]{:S(2)}, u32[]{:S(2)}) collective-permute-start(f32[10,1,128]{2,1,0:T(1,128)S(1)} %get-tuple-element.347), channel_id=1, source_target_pairs={{1,0},{2,1},{3,2},{4,3},{5,4},{6,5},{7,6},{0,7},{9,8},{10,9},{11,1... | collective-permute-start | bytes 15368 | tf_op jit(solution)/shard_map/ppermute | solution.py:27
  205.9 1.2 collective-permute-start.10
  207.2 6.2 %collective-permute-start.13 = (f32[1,8,128]{2,1,0:T(8,128)S(1)}, f32[1,8,128]{2,1,0:T(8,128)S(1)}, u32[]{:S(2)}, u32[]{:S(2)}) collective-permute-start(f32[1,8,128]{2,1,0:T(8,128)S(1)} %get-tuple-element.353), channel_id=1, source_target_pairs={{8,0},{16,8},{24,16},{32,24},{40,32},{48,40},{56,48},{64,56},{72,6... | collective-permute-start | bytes 12296 | tf_op jit(solution)/shard_map/ppermute | solution.py:27
  209.8 7.7 %collective-permute-start.12 = (f32[1,8,128]{2,1,0:T(8,128)S(1)}, f32[1,8,128]{2,1,0:T(8,128)S(1)}, u32[]{:S(2)}, u32[]{:S(2)}) collective-permute-start(f32[1,8,128]{2,1,0:T(8,128)S(1)} %get-tuple-element.352), channel_id=1, source_target_pairs={{0,8},{8,16},{16,24},{24,32},{32,40},{40,48},{48,56},{56,64},{64,7... | collective-permute-start | bytes 12296 | tf_op jit(solution)/shard_map/ppermute | solution.py:24
  217.5 5.9 %collective-permute-start.15 = (f32[10,1,128]{2,1,0:T(1,128)S(1)}, f32[10,1,128]{2,1,0:T(1,128)S(1)}, u32[]{:S(2)}, u32[]{:S(2)}) collective-permute-start(f32[10,1,128]{2,1,0:T(1,128)S(1)} %get-tuple-element.345), channel_id=1, source_target_pairs={{1,0},{2,1},{3,2},{4,3},{5,4},{6,5},{7,6},{0,7},{9,8},{10,9},{11,1... | collective-permute-start | bytes 15368 | tf_op jit(solution)/shard_map/ppermute | solution.py:27
  222.5 1.2 collective-permute-start.14
  223.9 6.9 %collective-permute-start.17 = (f32[1,8,128]{2,1,0:T(8,128)S(1)}, f32[1,8,128]{2,1,0:T(8,128)S(1)}, u32[]{:S(2)}, u32[]{:S(2)}) collective-permute-start(f32[1,8,128]{2,1,0:T(8,128)S(1)} %get-tuple-element.351), channel_id=1, source_target_pairs={{8,0},{16,8},{24,16},{32,24},{40,32},{48,40},{56,48},{64,56},{72,6... | collective-permute-start | bytes 12296 | tf_op jit(solution)/shard_map/ppermute | solution.py:27
  225.9 7.7 %collective-permute-start.16 = (f32[1,8,128]{2,1,0:T(8,128)S(1)}, f32[1,8,128]{2,1,0:T(8,128)S(1)}, u32[]{:S(2)}, u32[]{:S(2)}) collective-permute-start(f32[1,8,128]{2,1,0:T(8,128)S(1)} %get-tuple-element.350), channel_id=1, source_target_pairs={{0,8},{8,16},{16,24},{24,32},{32,40},{40,48},{48,56},{56,64},{64,7... | collective-permute-start | bytes 12296 | tf_op jit(solution)/shard_map/ppermute | solution.py:24
  233.5 5.1 %collective-permute-start.19 = (f32[10,1,128]{2,1,0:T(1,128)S(1)}, f32[10,1,128]{2,1,0:T(1,128)S(1)}, u32[]{:S(2)}, u32[]{:S(2)}) collective-permute-start(f32[10,1,128]{2,1,0:T(1,128)S(1)} %get-tuple-element.343), channel_id=1, source_target_pairs={{1,0},{2,1},{3,2},{4,3},{5,4},{6,5},{7,6},{0,7},{9,8},{10,9},{11,1... | collective-permute-start | bytes 15368 | tf_op jit(solution)/shard_map/ppermute | solution.py:27
  237.8 1.2 collective-permute-start.18
  (7 other events, 463.4 us)
where the time goes:
time: 448 us; the launch traced here: 444 us
  blocking collectives  202 us (45%)
  between operations  93.8 us (21%)
  starting transfers between devices  63.8 us (14%)
  other arithmetic  37.4 us (8%)
  waiting for transfers between devices  20.8 us (5%)
  local copies, waits for them, and re-layouts  20.3 us (5%)
  matrix products  6.24 us (1%)
    pmax x1, blocking collectives, on_device(): fastest = lax.pmax(jnp.max(jnp.abs(velocity)), ('axial', 'azim'))  101 us
    psum x1, blocking collectives, solve_pressure(): total = lax.psum(local, ('axial', 'azim'))  101 us
    ppermute x10, starting transfers between devices, extended(): lax.ppermute(lax.slice_in_dim(block, 0, width, axis=dim), axis, backward)  43.3 us
    ppermute x10, waiting for transfers between devices, extended(): lax.ppermute(lax.slice_in_dim(block, block.shape[dim] - width, None, axis...  16.9 us
    ppermute x10, starting transfers between devices, extended(): lax.ppermute(lax.slice_in_dim(block, block.shape[dim] - width, None, axis...  16.1 us
    mul x8, other arithmetic, evaporate(): sources = jnp.stack([heat_source * alive_mask, lost_mass * alive_mask])  11.7 us
    another operation x1, local copies, waits for them, and re-layouts, solve_pressure(): local = jnp.stack([jnp.sum(basis[i] * basis[j]) for i, j in pairs])  9.33 us
  transfers between devices with their start and end apart: 24, of which 11 were waited for; matrix products, arithmetic and copies ran while one was open for 11% of the time, Pallas kernels for 0%

commit v1 on v0

--- a/solution.py
+++ b/solution.py
@@ -155,7 +155,7 @@
     size = ITERS + 1
     pairs = [(i, j) for i in range(size) for j in range(i, size)]
     local = jnp.stack([jnp.sum(basis[i] * basis[j]) for i, j in pairs])
-    total = lax.psum(local, ("axial", "azim"))
+    total = lax.psum(lax.psum(local, "azim"), "axial")
     gram = [[None] * size for _ in range(size)]
     for n, (i, j) in enumerate(pairs):
         gram[i][j] = total[n]

time: 448 us -> 500 us (1.12)
  the two profiles are of different devices: /device:TPU:1 before, /device:TPU:2 now
where the time goes in v1:
time: 500 us; the launch traced here: 496 us
  blocking collectives  259 us (52%)
  between operations  93.8 us (19%)
  starting transfers between devices  52.2 us (10%)
  other arithmetic  37.4 us (7%)
  waiting for transfers between devices  26.4 us (5%)
  local copies, waits for them, and re-layouts  20.3 us (4%)
  matrix products  6.24 us (1%)
    psum x2, blocking collectives, solve_pressure(): total = lax.psum(lax.psum(local, 'azim'), 'axial')  154 us
    pmax x1, blocking collectives, on_device(): fastest = lax.pmax(jnp.max(jnp.abs(velocity)), ('axial', 'azim'))  106 us
    ppermute x10, starting transfers between devices, extended(): lax.ppermute(lax.slice_in_dim(block, 0, width, axis=dim), axis, backward)  24.5 us
    ppermute x10, waiting for transfers between devices, extended(): lax.ppermute(lax.slice_in_dim(block, block.shape[dim] - width, None, axis...  21.5 us
    ppermute x10, starting transfers between devices, extended(): lax.ppermute(lax.slice_in_dim(block, block.shape[dim] - width, None, axis...  15 us
    mul x8, other arithmetic, evaporate(): sources = jnp.stack([heat_source * alive_mask, lost_mass * alive_mask])  11.7 us
  transfers between devices with their start and end apart: 24, of which 13 were waited for; matrix products, arithmetic and copies ran while one was open for 10% of the time, Pallas kernels for 0%

profile of v1, /device:TPU:2, one launch (start us, length us, event | category | flops | bytes accessed | tf_op | source)
XLA Modules:
  0.0 496.2 jit_solution(7810636607284380067)
XLA Ops:
  1.6 3.4 collective-permute-start
  5.0 6.3 %collective-permute-start.1 = (f32[14,2,8,128]{3,2,1,0:T(8,128)S(1)}, f32[14,2,8,128]{3,2,1,0:T(8,128)S(1)}, u32[]{:S(2)}, u32[]{:S(2)}) collective-permute-start(f32[14,2,8,128]{3,2,1,0:T(8,128)S(1)} %get-tuple-element.334), channel_id=1, source_target_pairs={{8,0},{16,8},{24,16},{32,24},{40,32},{48,40},{56,48},{64,56},{72,6... | collective-permute-start | bytes 344072 | tf_op jit(solution)/shard_map/ppermute | solution.py:27
  13.8 105.7 %pmax.7 = f32[]{:T(128)} all-reduce(f32[]{:T(128)} %abs_reduce_fusion), channel_id=1, replica_groups=mesh['axial'=64,'azim'=8] {'axial','azim'}, use_global_device_ids=true, to_apply=%region_1.0 | all-reduce | flops 1 | bytes 8 | tf_op jit(solution)/shard_map/pmax | solution.py:220
  121.0 31.6 %while.18 = (s32[]{:T(128)}, f32[64,256]{1,0:T(8,128)S(1)}, f32[8,2048]{1,0:T(8,128)S(1)}, s32[2048]{0:T(1024)}, s32[]{:T(128)}, /*index=5*/f32[8,2048]{1,0:T(8,...) while((s32[]{:T(128)}, f32[64,256]{1,0:T(8,128)S(1)}, ...), condition=%wide.region_4.5_spmd.clone, body=%wide.region_2.4_spmd.clone.sunk | while | flops 353384960 | bytes 5411153 | solution.py:262
  155.5 2.9 collective-permute-start.22
  158.4 2.6 collective-permute-start.21
  162.4 2.4 collective-permute-done.3
  164.8 3.1 collective-permute-done.2
  169.8 2.7 copy.247
  175.4 3.2 collective-permute-start.5
  178.6 2.6 collective-permute-start.4
  181.3 3.0 collective-permute-done.4
  185.7 7.2 %collective-permute-start.20 = (f32[8,64]{1,0:T(8,128)S(1)}, f32[8,64]{1,0:T(8,128)S(1)}, u32[]{:S(2)}, u32[]{:S(2)}) collective-permute-start(f32[8,64]{1,0:T(8,128)S(1)} %get-tuple-element.358), channel_id=1, source_target_pairs={{8,0},{16,8},{24,16},{32,24},{40,32},{48,40},{56,48},{64,56},{72,6... | collective-permute-start | bytes 6152 | tf_op jit(solution)/shard_map/ppermute | solution.py:35
  193.1 2.9 collective-permute-start.9
  196.1 2.9 collective-permute-start.8
  203.4 2.9 collective-permute-done.10
  206.5 4.9 collective-permute-start.13
  214.3 2.6 collective-permute-done.12
  218.3 2.9 collective-permute-done.14
  221.4 6.5 %collective-permute-start.17 = (f32[1,8,128]{2,1,0:T(8,128)S(1)}, f32[1,8,128]{2,1,0:T(8,128)S(1)}, u32[]{:S(2)}, u32[]{:S(2)}) collective-permute-start(f32[1,8,128]{2,1,0:T(8,128)S(1)} %get-tuple-element.351), channel_id=1, source_target_pairs={{8,0},{16,8},{24,16},{32,24},{40,32},{48,40},{56,48},{64,56},{72,6... | collective-permute-start | bytes 12296 | tf_op jit(solution)/shard_map/ppermute | solution.py:27
  234.8 2.9 collective-permute-done.18
  238.7 9.3 %stack.131 = f32[15]{0:T(128)S(1)} concatenate(f32[1]{0:T(128)} %bitcast.15, f32[1]{0:T(128)} %bitcast.16, f32[1]{0:T(128)} %bitcast.17, f32[1]{0:T(128)} %bitcast.18, f32[1]{0:T(128)} %bitcast.19, f32[1]{0:T(128)} %bitcast.20, f32[1]{0:T(128)} %bitcast.21, f32[1]{0:T(128)} %bitcast.22, f32[1]{0:T(128)} %bitcast.23, f32[1]{0:T(128)} %bitcast.24, f32[1]{0:T(128)} %bitcast.25, ...), dimensions={0} | concatenate | bytes 120 | tf_op jit(solution)/shard_map/stack | solution.py:157
  248.0 12.4 %psum.14 = f32[15]{0:T(128)S(1)} all-reduce(f32[15]{0:T(128)S(1)} %stack.131), channel_id=1, replica_groups=mesh['axial'=64,'azim'=8] {'azim'}, use_global_device_ids=true, to_apply=%region_20.21 | all-reduce | flops 15 | bytes 120 | tf_op jit(solution)/shard_map/psum | solution.py:158
  261.2 141.3 %psum.15 = f32[15]{0:T(128)S(1)} all-reduce(f32[15]{0:T(128)S(1)} %psum.14), channel_id=1, replica_groups=mesh['axial'=64,'azim'=8] {'axial'}, use_global_device_ids=true, to_apply=%region_21.22 | all-reduce | flops 15 | bytes 120 | tf_op jit(solution)/shard_map/psum | solution.py:158
  (168 shorter events, 64.9 us)
Async XLA Ops:
  1.6 160.1 %collective-permute-start = (f32[14,2,8,128]{3,2,1,0:T(8,128)S(1)}, f32[14,2,8,128]{3,2,1,0:T(8,128)S(1)}, u32[]{:S(2)}, u32[]{:S(2)}) collective-permute-start(f32[14,2,8,128]{3,2,1,0:T(8,128)S(1)} %get-tuple-element.335), channel_id=1, source_target_pairs={{0,8},{8,16},{16,24},{24,32},{32,40},{40,48},{48,56},{56,64},{64,7... | collective-permute-start | bytes 344072 | tf_op jit(solution)/shard_map/ppermute | solution.py:24
  5.0 156.7 %collective-permute-start.1 = (f32[14,2,8,128]{3,2,1,0:T(8,128)S(1)}, f32[14,2,8,128]{3,2,1,0:T(8,128)S(1)}, u32[]{:S(2)}, u32[]{:S(2)}) collective-permute-start(f32[14,2,8,128]{3,2,1,0:T(8,128)S(1)} %get-tuple-element.334), channel_id=1, source_target_pairs={{8,0},{16,8},{24,16},{32,24},{40,32},{48,40},{56,48},{64,56},{72,6... | collective-permute-start | bytes 344072 | tf_op jit(solution)/shard_map/ppermute | solution.py:27
  155.4 40.6 %collective-permute-start.23 = (f32[8,64]{1,0:T(8,128)S(1)}, f32[8,64]{1,0:T(8,128)S(1)}, u32[]{:S(2)}, u32[]{:S(2)}) collective-permute-start(f32[8,64]{1,0:T(8,128)S(1)} %get-tuple-element.359), channel_id=1, source_target_pairs={{0,1},{1,2},{2,3},{3,4},{4,5},{5,6},{6,7},{7,0},{8,9},{9,10},{10,1... | collective-permute-start | bytes 6152 | tf_op jit(solution)/shard_map/ppermute | solution.py:40
  155.5 43.5 %collective-permute-start.22 = (f32[8,64]{1,0:T(8,128)S(1)}, f32[8,64]{1,0:T(8,128)S(1)}, u32[]{:S(2)}, u32[]{:S(2)}) collective-permute-start(f32[8,64]{1,0:T(8,128)S(1)} %get-tuple-element.360), channel_id=1, source_target_pairs={{0,7},{1,0},{2,1},{3,2},{4,3},{5,4},{6,5},{7,6},{8,15},{9,8},{10,9... | collective-permute-start | bytes 6152 | tf_op jit(solution)/shard_map/ppermute | solution.py:40
  158.4 40.6 %collective-permute-start.21 = (f32[8,64]{1,0:T(8,128)S(1)}, f32[8,64]{1,0:T(8,128)S(1)}, u32[]{:S(2)}, u32[]{:S(2)}) collective-permute-start(f32[8,64]{1,0:T(8,128)S(1)} %get-tuple-element.361), channel_id=1, source_target_pairs={{0,8},{8,16},{16,24},{24,32},{32,40},{40,48},{48,56},{56,64},{64,7... | collective-permute-start | bytes 6152 | tf_op jit(solution)/shard_map/ppermute | solution.py:35
  161.9 2.9 collective-permute-start.3
  161.9 6.1 %collective-permute-start.2 = (f32[14,12,2,128]{3,2,1,0:T(2,128)S(1)}, f32[14,12,2,128]{3,2,1,0:T(2,128)S(1)}, u32[]{:S(2)}, u32[]{:S(2)}) collective-permute-start(f32[14,12,2,128]{3,2,1,0:T(2,128)S(1)} %get-tuple-element.329), channel_id=1, source_target_pairs={{0,1},{1,2},{2,3},{3,4},{4,5},{5,6},{6,7},{7,0},{8,9},{9,10},{10,1... | collective-permute-start | bytes 516104 | tf_op jit(solution)/shard_map/ppermute | solution.py:24
  175.4 5.9 %collective-permute-start.5 = (f32[1,8,128]{2,1,0:T(8,128)S(1)}, f32[1,8,128]{2,1,0:T(8,128)S(1)}, u32[]{:S(2)}, u32[]{:S(2)}) collective-permute-start(f32[1,8,128]{2,1,0:T(8,128)S(1)} %get-tuple-element.357), channel_id=1, source_target_pairs={{8,0},{16,8},{24,16},{32,24},{40,32},{48,40},{56,48},{64,56},{72,6... | collective-permute-start | bytes 12296 | tf_op jit(solution)/shard_map/ppermute | solution.py:27
  178.6 5.7 %collective-permute-start.4 = (f32[1,8,128]{2,1,0:T(8,128)S(1)}, f32[1,8,128]{2,1,0:T(8,128)S(1)}, u32[]{:S(2)}, u32[]{:S(2)}) collective-permute-start(f32[1,8,128]{2,1,0:T(8,128)S(1)} %get-tuple-element.356), channel_id=1, source_target_pairs={{0,8},{8,16},{16,24},{24,32},{32,40},{40,48},{48,56},{56,64},{64,7... | collective-permute-start | bytes 12296 | tf_op jit(solution)/shard_map/ppermute | solution.py:24
  184.3 1.4 collective-permute-start.7
  184.3 8.6 %collective-permute-start.6 = (f32[10,1,128]{2,1,0:T(1,128)S(1)}, f32[10,1,128]{2,1,0:T(1,128)S(1)}, u32[]{:S(2)}, u32[]{:S(2)}) collective-permute-start(f32[10,1,128]{2,1,0:T(1,128)S(1)} %get-tuple-element.348), channel_id=1, source_target_pairs={{0,1},{1,2},{2,3},{3,4},{4,5},{5,6},{6,7},{7,0},{8,9},{9,10},{10,1... | collective-permute-start | bytes 15368 | tf_op jit(solution)/shard_map/ppermute | solution.py:24
  185.7 13.3 %collective-permute-start.20 = (f32[8,64]{1,0:T(8,128)S(1)}, f32[8,64]{1,0:T(8,128)S(1)}, u32[]{:S(2)}, u32[]{:S(2)}) collective-permute-start(f32[8,64]{1,0:T(8,128)S(1)} %get-tuple-element.358), channel_id=1, source_target_pairs={{8,0},{16,8},{24,16},{32,24},{40,32},{48,40},{56,48},{64,56},{72,6... | collective-permute-start | bytes 6152 | tf_op jit(solution)/shard_map/ppermute | solution.py:35
  193.1 6.5 %collective-permute-start.9 = (f32[1,8,128]{2,1,0:T(8,128)S(1)}, f32[1,8,128]{2,1,0:T(8,128)S(1)}, u32[]{:S(2)}, u32[]{:S(2)}) collective-permute-start(f32[1,8,128]{2,1,0:T(8,128)S(1)} %get-tuple-element.355), channel_id=1, source_target_pairs={{8,0},{16,8},{24,16},{32,24},{40,32},{48,40},{56,48},{64,56},{72,6... | collective-permute-start | bytes 12296 | tf_op jit(solution)/shard_map/ppermute | solution.py:27
  196.1 5.5 %collective-permute-start.8 = (f32[1,8,128]{2,1,0:T(8,128)S(1)}, f32[1,8,128]{2,1,0:T(8,128)S(1)}, u32[]{:S(2)}, u32[]{:S(2)}) collective-permute-start(f32[1,8,128]{2,1,0:T(8,128)S(1)} %get-tuple-element.354), channel_id=1, source_target_pairs={{0,8},{8,16},{16,24},{24,32},{32,40},{40,48},{48,56},{56,64},{64,7... | collective-permute-start | bytes 12296 | tf_op jit(solution)/shard_map/ppermute | solution.py:24
  201.6 1.8 collective-permute-start.11
  202.1 4.3 collective-permute-start.10
  206.5 7.8 %collective-permute-start.13 = (f32[1,8,128]{2,1,0:T(8,128)S(1)}, f32[1,8,128]{2,1,0:T(8,128)S(1)}, u32[]{:S(2)}, u32[]{:S(2)}) collective-permute-start(f32[1,8,128]{2,1,0:T(8,128)S(1)} %get-tuple-element.353), channel_id=1, source_target_pairs={{8,0},{16,8},{24,16},{32,24},{40,32},{48,40},{56,48},{64,56},{72,6... | collective-permute-start | bytes 12296 | tf_op jit(solution)/shard_map/ppermute | solution.py:27
  211.4 5.5 %collective-permute-start.12 = (f32[1,8,128]{2,1,0:T(8,128)S(1)}, f32[1,8,128]{2,1,0:T(8,128)S(1)}, u32[]{:S(2)}, u32[]{:S(2)}) collective-permute-start(f32[1,8,128]{2,1,0:T(8,128)S(1)} %get-tuple-element.352), channel_id=1, source_target_pairs={{0,8},{8,16},{16,24},{24,32},{32,40},{40,48},{48,56},{56,64},{64,7... | collective-permute-start | bytes 12296 | tf_op jit(solution)/shard_map/ppermute | solution.py:24
  216.9 1.4 collective-permute-start.15
  217.0 4.3 collective-permute-start.14
  221.4 10.1 %collective-permute-start.17 = (f32[1,8,128]{2,1,0:T(8,128)S(1)}, f32[1,8,128]{2,1,0:T(8,128)S(1)}, u32[]{:S(2)}, u32[]{:S(2)}) collective-permute-start(f32[1,8,128]{2,1,0:T(8,128)S(1)} %get-tuple-element.351), channel_id=1, source_target_pairs={{8,0},{16,8},{24,16},{32,24},{40,32},{48,40},{56,48},{64,56},{72,6... | collective-permute-start | bytes 12296 | tf_op jit(solution)/shard_map/ppermute | solution.py:27
  228.0 5.5 %collective-permute-start.16 = (f32[1,8,128]{2,1,0:T(8,128)S(1)}, f32[1,8,128]{2,1,0:T(8,128)S(1)}, u32[]{:S(2)}, u32[]{:S(2)}) collective-permute-start(f32[1,8,128]{2,1,0:T(8,128)S(1)} %get-tuple-element.350), channel_id=1, source_target_pairs={{0,8},{8,16},{16,24},{24,32},{32,40},{40,48},{48,56},{56,64},{64,7... | collective-permute-start | bytes 12296 | tf_op jit(solution)/shard_map/ppermute | solution.py:24
  233.5 1.4 collective-permute-start.19
  233.5 4.3 collective-permute-start.18
  (7 other events, 582.9 us)
